TPU v7x, 128 devices: a whole 4x4x4 slice. The times are simulated.
128 devices in a mesh: row: 16 (over z, x_hi, core), col: 8 (over y, x_lo).
Axes of the slice: x: 4 (x_hi: 2, x_lo: 2; x = x_hi * 2 + x_lo), y: 4, z: 4, core: 2. Of those that a mesh axis runs over, the one named last changes fastest.
Arguments:
- momentum_shards: bfloat16 [6656, 18432], P(('row', 'col')), may hold values from -0.078125 to 0.078125
- shard_starts: int32 [128], replicated, may hold values from 0 to 3568, as said below
Outputs:
- update_shards: bfloat16 [6656, 18432], P(('row', 'col'))
Inputs may be any that keep to these rules, and one draw needn't show every extreme that they name: `shard_starts`: starts never fall and the first is 0; shard d starts within 12 rows of d * 28, and the last one exactly 12 rows after it. Every shard has at most 52 rows and some shard has exactly 52; the 8 shards of one index of row hold at most 248 rows together, and on some index exactly 248.
All inputs are finite; a program needn't handle non-finite values.
Results may differ from a plain program's by a relative error of at most 0.02.
Values may be sent and summed in bfloat16 or wider, within the bound.
A program may use at most 128 MiB of HBM per device.

v0:
```python
import math

import jax
import jax.numpy as jnp
from jax import lax
from jax.sharding import PartitionSpec as P

M = 3584
N = 18432


coef_one = 3.4445
coef_two = -4.775
coef_three = 2.0315


def in_blocks(value, dim, size):
    shape = value.shape
    tiles = value.reshape(*shape[:dim], size, shape[dim] // size, *shape[dim + 1 :])
    return jnp.moveaxis(tiles, dim, 0)


def summed_on_arrival(value, axis, dim):
    size = lax.axis_size(axis)
    tiles = lax.all_to_all(in_blocks(value, dim, size), axis, 0, 0, tiled=True)
    return jnp.sum(tiles.astype(jnp.float32), axis=0)


def laid_out(tiles, dim):
    shape = list(tiles.shape[1:])
    shape[dim] *= tiles.shape[0]
    return jnp.moveaxis(tiles, 0, dim).reshape(shape)


def sent_to_all(value, axis):
    copies = jnp.broadcast_to(value, (lax.axis_size(axis), *value.shape))
    return lax.all_to_all(copies, axis, split_axis=0, concat_axis=0, tiled=True)


def gather_directly(value, axis, dim):
    return laid_out(sent_to_all(value, axis), dim)


def packing(shard_starts, row_block, col_count, shard_rows, window):
    shard_ends = jnp.concatenate([shard_starts[1:], jnp.full((1,), M, jnp.int32)])
    first_starts = lax.dynamic_slice_in_dim(shard_starts, row_block * col_count, col_count)
    last_ends = lax.dynamic_slice_in_dim(shard_ends, row_block * col_count, col_count)
    slot_index = jnp.arange(col_count * shard_rows, dtype=jnp.int32)
    member = slot_index // shard_rows
    offset = slot_index % shard_rows
    pick = member[:, None] == jnp.arange(col_count, dtype=jnp.int32)[None, :]
    shard_begin = jnp.sum(jnp.where(pick, first_starts[None, :], 0), axis=1)
    length = jnp.sum(jnp.where(pick, (last_ends - first_starts)[None, :], 0), axis=1)
    target = shard_begin - first_starts[0] + offset
    is_valid = offset < length
    window_rows = jnp.arange(window, dtype=jnp.int32)
    return ((window_rows[:, None] == target[None, :]) & is_valid[None, :]).astype(jnp.bfloat16)


def body(momentum_shards, shard_starts):
    col_count = lax.axis_size("col")
    row_count = lax.axis_size("row")
    shard_rows = momentum_shards.shape[0]
    mean_rows = M // (row_count * col_count)
    jitter = 4 * (mean_rows // 8)
    window = col_count * mean_rows + 2 * jitter
    packer = packing(shard_starts, lax.axis_index("row"), col_count, shard_rows, window)
    columns = lax.all_to_all(momentum_shards, "col", split_axis=1, concat_axis=0, tiled=True)
    local_tile = jnp.dot(packer, columns, preferred_element_type=jnp.float32).astype(jnp.bfloat16)
    col_panel = lax.all_gather(local_tile, "row", axis=0, tiled=True)
    own_block = summed_on_arrival(
        lax.dot_general(
            col_panel, local_tile, (((1,), (1,)), ((), ())), preferred_element_type=jnp.float32
        ).astype(jnp.bfloat16),
        "col",
        0,
    ).astype(jnp.bfloat16)
    across = lax.all_gather(own_block, "row", axis=1, tiled=True)
    square_own = summed_on_arrival(
        lax.dot_general(
            across, own_block, (((0,), (0,)), ((), ())), preferred_element_type=jnp.float32
        ).astype(jnp.bfloat16),
        "col",
        0,
    )
    poly_own = (coef_two * own_block.astype(jnp.float32) + coef_three * square_own).astype(
        jnp.bfloat16
    )
    poly_block = gather_directly(poly_own, "col", 0)
    mixed_part = lax.dot_general(
        poly_block, col_panel, (((0,), (0,)), ((), ())), preferred_element_type=jnp.float32
    )
    update = (math.sqrt(N) * (coef_one * local_tile.astype(jnp.float32) + mixed_part)).astype(
        jnp.bfloat16
    )
    back_rows = lax.dot_general(
        packer, update, (((0,), (0,)), ((), ())), preferred_element_type=jnp.float32
    ).astype(jnp.bfloat16)
    return lax.all_to_all(back_rows, "col", split_axis=0, concat_axis=1, tiled=True)


def solution(mesh):
    in_specs = (P(("row", "col"), None), P())
    out_specs = P(("row", "col"), None)
    return jax.shard_map(body, mesh=mesh, in_specs=in_specs, out_specs=out_specs, check_vma=False)
```

profile of v0, /device:TPU:1, one launch (start us, length us, event | category | flops | bytes accessed | tf_op | source)
XLA Modules:
  0.0 385.9 jit_solution(3728973360433823546)
XLA Ops:
  6.5 1.9 copy.23
  8.5 0.1 slice.8
  8.6 1.6 copy.14
  10.2 6.1 %all-to-all-start = ((bf16[52,8,2304]{2,0,1:T(8,128)(2,1)}), bf16[52,8,2304]{2,0,1:T(8,128)(2,1)S(1)}, u32[]{:S(2)}, u32[]{:S(2)}) async-start(bf16[52,8,2304]{2,0,1:T(8,128)(2,1)} %copy.14), calls=%async_computation | async-start | bytes 4128768 | tf_op jit(solution)/shard_map/all_to_all | solution.py:68
  16.4 0.1 pad_add_fusion
  16.6 0.1 select_reduce_fusion
  16.8 25.3 %all-to-all-done = bf16[52,8,2304]{2,0,1:T(8,128)(2,1)S(1)} async-done(((bf16[52,8,2304]{2,0,1:T(8,128)(2,1)}), bf16[52,8,2304]{2,0,1:T(8,128)(2,1)S(1)}, u32[]{:S(2)}, u32[]{:S(2)}) %all-to-all-start) | async-done | bytes 1916960 | tf_op jit(solution)/shard_map/all_to_all | solution.py:68
  42.1 1.4 all_to_all.40
  43.5 3.3 convolution_convert_fusion.3
  46.9 117.7 %all-gather.3.cloned.1.call-done = bf16[3968,2304]{1,0:T(8,128)(2,1)} async-done(((bf16[248,2304]{1,0:T(8,128)(2,1)}), bf16[3968,2304]{1,0:T(8,128)(2,1)}) %all-gather.3.cloned.1.call-update) | async-done | bytes 18284560 | tf_op jit(solution)/shard_map/all_gather | solution.py:70
  164.7 12.8 %convolution_convert_fusion.1 = bf16[3968,248]{0,1:T(8,128)(2,1)} fusion(bf16[3968,2304]{1,0:T(8,128)(2,1)} %all-gather.3.cloned.1.call-done, bf16[248,2304]{1,0:T(8,128)(2,1)} %convolution_convert_fusion.3), kind=kOutput, calls=%fused_computation.1 | convolution fusion | flops 4535550976 | bytes 21395456 | tf_op jit(solution)/shard_map/dot_general | solution.py:72
  177.4 5.6 %reshape.48 = bf16[8,496,248]{1,0,2:T(8,128)(2,1)S(1)} reshape(bf16[3968,248]{0,1:T(8,128)(2,1)} %convolution_convert_fusion.1) | data formatting | bytes 3936256 | tf_op jit(solution)/shard_map/reshape | solution.py:19
  183.0 0.7 copy.15
  183.7 29.5 %all_to_all.53 = bf16[8,496,248]{1,2,0:T(8,128)(2,1)S(1)} all-to-all(bf16[8,496,248]{1,2,0:T(8,128)(2,1)S(1)} %copy.15), channel_id=1, replica_groups=mesh['row'=16,'col'=8] {'col'}, dimensions={0} | all-to-all | bytes 3936256 | tf_op jit(solution)/shard_map/all_to_all | solution.py:25
  213.2 1.1 reduce_sum.41
  214.3 52.6 %all-gather.5.cloned.1.call-done = bf16[496,3968]{0,1:T(8,128)(2,1)} async-done(((bf16[496,248]{0,1:T(8,128)(2,1)}), bf16[496,3968]{0,1:T(8,128)(2,1)}) %all-gather.5.cloned.1.call-update) | async-done | bytes 3936272 | tf_op jit(solution)/shard_map/all_gather | solution.py:78
  266.8 4.7 %convolution_convert_fusion = bf16[3968,248]{0,1:T(8,128)(2,1)} fusion(bf16[496,3968]{0,1:T(8,128)(2,1)} %all-gather.5.cloned.1.call-done, bf16[496,248]{0,1:T(8,128)(2,1)} %reduce_sum.41), kind=kOutput, calls=%fused_computation | convolution fusion | flops 977175552 | bytes 6150400 | tf_op jit(solution)/shard_map/dot_general | solution.py:80
  271.6 5.6 %reshape.49 = bf16[8,496,248]{1,0,2:T(8,128)(2,1)S(1)} reshape(bf16[3968,248]{0,1:T(8,128)(2,1)} %convolution_convert_fusion) | data formatting | bytes 3936256 | tf_op jit(solution)/shard_map/reshape | solution.py:19
  277.2 0.7 copy.17
  277.8 29.5 %all_to_all.54 = bf16[8,496,248]{1,2,0:T(8,128)(2,1)S(1)} all-to-all(bf16[8,496,248]{1,2,0:T(8,128)(2,1)S(1)} %copy.17), channel_id=1, replica_groups=mesh['row'=16,'col'=8] {'col'}, dimensions={0} | all-to-all | bytes 3936256 | tf_op jit(solution)/shard_map/all_to_all | solution.py:25
  307.3 0.3 convert_reduce_fusion
  307.7 0.6 copy-done
  308.3 0.1 add_convert_fusion
  308.4 0.1 copy.19
  308.5 0.1 broadcast_in_dim.31
  308.7 27.9 %all_to_all.55 = bf16[8,496,248]{2,1,0:T(8,128)(2,1)S(1)} all-to-all(bf16[8,496,248]{2,1,0:T(8,128)(2,1)S(1)} %broadcast_in_dim.31), channel_id=1, replica_groups=mesh['row'=16,'col'=8] {'col'}, dimensions={0} | all-to-all | bytes 3936256 | tf_op jit(solution)/shard_map/all_to_all | solution.py:37
  336.6 11.1 %convolution_convert_fusion.2 = bf16[416,2304]{1,0:T(8,128)(2,1)} fusion(s32[416]{0:T(512)S(1)} %subtract_add_fusion, pred[416]{0:T(512)(128)(4,1)S(1)} %fusion.16, bf16[3968,248]{1,0:T(8,128)(2,1)S(1)} %bitcast.27, bf16[3968,2304]{1,0:T(8,128)(2,1)} %all-gather.3.cloned.1.call-done, bf16[248,2304]{1,0:T(8,128)(2,1)S(1)} %copy-done.1), kind=kOutput, calls=%fused_computation.2 | convolution fusion | flops 5013986816 | bytes 23314464 | tf_op jit(solution)/shard_map/dot_general | solution.py:96
  347.7 1.7 all_to_all.44
  349.4 27.5 %all_to_all.56 = bf16[8,52,2304]{2,1,0:T(8,128)(2,1)S(1)} all-to-all(bf16[8,52,2304]{2,1,0:T(8,128)(2,1)S(1)} %all_to_all.44), channel_id=1, replica_groups=mesh['row'=16,'col'=8] {'col'}, dimensions={0} | all-to-all | bytes 3833856 | tf_op jit(solution)/shard_map/all_to_all | solution.py:99
  376.9 0.3 copy.20
  377.3 0.1 pad.2
  377.4 1.7 copy.24
  (14 shorter events, 0.3 us)
Async XLA Ops:
  10.2 6.1 %copy-start.2 = (s32[128]{0:T(128)S(1)}, s32[128]{0:T(128)}, u32[]{:S(2)}) copy-start(s32[128]{0:T(128)} %param.3) | copy-start | bytes 1540
  10.2 31.8 %all-to-all-start = ((bf16[52,8,2304]{2,0,1:T(8,128)(2,1)}), bf16[52,8,2304]{2,0,1:T(8,128)(2,1)S(1)}, u32[]{:S(2)}, u32[]{:S(2)}) async-start(bf16[52,8,2304]{2,0,1:T(8,128)(2,1)} %copy.14), calls=%async_computation | async-start | bytes 4128768 | tf_op jit(solution)/shard_map/all_to_all | solution.py:68
  16.3 148.4 %all-gather.3.cloned.1.call-start = ((), (), s32[]{:S(2)}) async-start(), calls=%async_computation.5 | async-start | bytes 19427328 | tf_op jit(solution)/shard_map/all_gather | solution.py:70
  46.9 220.0 %all-gather.5.cloned.1.call-start = ((), (), s32[]{:S(2)}) async-start(), calls=%async_computation.6 | async-start | bytes 4317184 | tf_op jit(solution)/shard_map/all_gather | solution.py:78
  307.3 0.9 copy-start
  308.6 27.9 %copy-start.1 = (bf16[248,2304]{1,0:T(8,128)(2,1)S(1)}, bf16[248,2304]{1,0:T(8,128)(2,1)}, u32[]{:S(2)}) copy-start(bf16[248,2304]{1,0:T(8,128)(2,1)} %convolution_convert_fusion.3) | copy-start | bytes 3428356
Sparse Core Ops, SparseCore 0:
  47.0 117.6 all-gather.2
  214.4 52.3 all-gather.4
where the time goes:
time: 388 us; the launch traced here: 386 us
  waiting for transfers between devices  196 us (51%)
  blocking collectives  114 us (29%)
  matrix products  32 us (8%)
  local copies, waits for them, and re-layouts  22.3 us (6%)
  between operations  13.5 us (3%)
  starting transfers between devices  6.15 us (2%)
    all_gather x1, waiting for transfers between devices, body(): col_panel = lax.all_gather(local_tile, 'row', axis=0, tiled=True)  118 us
    all_to_all x2, blocking collectives, summed_on_arrival(): tiles = lax.all_to_all(in_blocks(value, dim, size), axis, 0, 0, tiled=True)  59 us
    all_gather x1, waiting for transfers between devices, body(): across = lax.all_gather(own_block, 'row', axis=1, tiled=True)  52.6 us
    all_to_all x1, blocking collectives, sent_to_all(): return lax.all_to_all(copies, axis, split_axis=0, concat_axis=0, tiled=True)  27.9 us
    all_to_all x1, blocking collectives, body(): lax.all_to_all(back_rows, 'col', split_axis=0, concat_axis=1, tiled=True)  27.5 us
    all_to_all x1, waiting for transfers between devices, body(): lax.all_to_all(momentum_shards, 'col', split_axis=1, concat_axis=0, tiled...  25.3 us
    dot_general x1, matrix products, body(): lax.dot_general(col_panel, local_tile, (((1,), (1,)), ((), ())), preferre...  12.8 us
    reshape x4, local copies, waits for them, and re-layouts, in_blocks(): value.reshape(*shape[:dim], size, shape[dim] // size, *shape[dim + 1:])  12.5 us
  transfers between devices with their start and end apart: 3, of which 3 were waited for; matrix products, arithmetic and copies ran while one was open for 0% of the time, Pallas kernels for 0%

commit v1 on v0

v1 whole, which is shorter than its diff:
```python
import math

import jax
import jax.numpy as jnp
from jax import lax
from jax.experimental import pallas as pl
from jax.experimental.pallas import tpu as pltpu
from jax.sharding import PartitionSpec as P

M = 3584
N = 18432
SHARDS = 128
CAP = 52
SLOT = 64
GROUPS = 8
MEMBERS = 16
WIN = 480
HALF = WIN // 2
PIECE = N // MEMBERS
WA = 640
WB = PIECE - WA
SLOTS = MEMBERS * SLOT
MESH = pl.DeviceIdType.MESH

coef_one = 3.4445
coef_two = -4.775
coef_three = 2.0315

GATHER = 23
ID_IN_A = 0
ID_IN_B = 16
ID_OUT_A = 32
ID_OUT_B = 48
ID_X = 64
ID_GL = ID_X + GATHER
ID_GR = ID_GL + GATHER
ID_P = ID_GR + GATHER
ID_MATE = ID_P + GATHER
ID_RS = ID_MATE + 8
ID_GRM = ID_RS + 8
ID_PM = ID_GRM + 8
IDS = ID_PM + 8

STEP_RING = (0, 3, 1, 0, 2, 3, 1, 2)
STEP_PAIR = (0, 0, 0, 1, 0, 1, 1, 1)


def pick(values, index):
    out = jnp.int32(values[0])
    for i, value in enumerate(values):
        if i and value != values[0]:
            out = jnp.where(index == i, jnp.int32(value), out)
    return out


def dot_nt(a, b):
    return lax.dot_general(a, b, (((1,), (1,)), ((), ())), preferred_element_type=jnp.float32)


def dot_nn(a, b):
    return lax.dot_general(a, b, (((1,), (0,)), ((), ())), preferred_element_type=jnp.float32)


class Gather:
    def __init__(self, net, base, ring, pair, ref, dev):
        self.net, self.base, self.ring, self.pair, self.ref, self.dev = net, base, ring, pair, ref, dev

    def at(self, part, half, step, other):
        return self.ref(part, half, (self.ring + step) % 4, (self.pair + other) % 2)

    def to(self, step, other):
        return self.dev((self.ring + step) % 4, (self.pair + other) % 2)

    def send(self, i, part, half, step, other, dest):
        ref = self.at(part, half, step, other)
        self.net.push(ref, ref, self.base + i, self.to(*dest))

    def wait(self, i, part, half, step, other):
        self.net.arrived(self.at(part, half, step, other), self.base + i)

    def ring_sends(self, part, s):
        base = 13 if part else 1 + s * 4
        for direction, half in ((0, 0), (1, 1), (0, 1), (1, 0)):
            self.send(base + direction * 2 + half, part, half, 0, s, (1 - 2 * direction, 0))

    def start_a(self):
        self.send(0, 0, None, 0, 0, (0, 1))
        self.ring_sends(0, 0)

    def start_b(self):
        self.ring_sends(1, 0)
        self.send(19, 1, None, 0, 0, (0, 1))

    def on_pair_a(self):
        self.wait(0, 0, None, 0, 1)
        self.ring_sends(0, 1)

    def on_ring(self, part, s):
        base = 13 if part else 1 + s * 4
        fwd = 17 if part else 9 + s * 2
        self.wait(base, part, 0, -1, s)
        self.send(fwd, part, 0, -1, s, (1, 0))
        self.wait(base + 3, part, 1, 1, s)
        self.send(fwd + 1, part, 1, 1, s, (-1, 0))
        self.wait(base + 1, part, 1, -1, s)
        self.wait(base + 2, part, 0, 1, s)
        if part:
            self.send(20, 1, None, -1, 0, (0, 1))
            self.send(21, 1, None, 1, 0, (0, 1))

    def on_far(self, part, s):
        fwd = 17 if part else 9 + s * 2
        self.wait(fwd, part, 0, 2, s)
        self.wait(fwd + 1, part, 1, 2, s)
        if part:
            self.send(22, 1, None, 2, 0, (0, 1))

    def on_pair_b(self, j):
        self.wait(19 + j, 1, None, (0, -1, 1, 2)[j], 1)

    def before(self, t):
        if t == 1:
            self.on_ring(0, 0)
            self.on_ring(1, 0)
            self.on_pair_a()
        elif t == 3:
            self.on_pair_b(0)
        elif t == 4:
            self.on_far(0, 0)
            self.on_far(1, 0)
        elif t == 5:
            self.on_ring(0, 1)
            self.on_pair_b(1)
        elif t == 6:
            self.on_pair_b(2)
        elif t == 7:
            self.on_far(0, 1)
            self.on_pair_b(3)

    def drain(self):
        for i, part, half in (
            [(0, 0, None)]
            + [(1 + n, 0, n % 2) for n in range(8)]
            + [(9 + n, 0, n % 2) for n in range(4)]
            + [(13 + n, 1, n % 2) for n in range(4)]
            + [(17 + n, 1, n % 2) for n in range(2)]
            + [(19 + n, 1, None) for n in range(4)]
        ):
            self.net.sent(self.at(part, half, 0, 0), self.base + i)


class Net:
    def __init__(self, send, recv, me):
        self.send, self.recv, self.me = send, recv, me

    def copy(self, src, dst, i, dev):
        return pltpu.make_async_remote_copy(
            src_ref=src, dst_ref=dst, send_sem=self.send.at[i], recv_sem=self.recv.at[i], device_id=dev, device_id_type=MESH
        )

    def push(self, src, dst, i, dev):
        self.copy(src, dst, i, dev).start()

    def arrived(self, dst, i):
        self.copy(dst, dst, i, self.me).wait_recv()

    def sent(self, src, i):
        self.copy(src, src, i, self.me).wait_send()


def kernel(
    starts, shard, out, ra, rb, fa, fb, pack, unpack, xa, xb, gown, gsnd, gmate, rsnd, rrcv, rsum, gl, gr, pb, acc, sq, sa, sb, send, recv, local
):
    row, col = lax.axis_index("row"), lax.axis_index("col")
    z, h, c = row // 4, (row // 2) % 2, row % 2
    y, q = col // 2, (col % 2 + (row // 2) % 2) % 2
    grp, k, pos = row // 2, y * 2 + q, c * 8 + col

    def device(z_, h_, c_, y_, q_):
        return ((z_ * 2 + h_) * 2 + c_, y_ * 2 + (q_ + h_) % 2)

    def member(p):
        c_, col_ = p // 8, p % 8
        return (grp * 2 + c_, col_), ((col_ // 2) * 2 + (col_ % 2 + h) % 2) * 2 + c_

    mate = device(z, h, 1 - c, y, q)
    net = Net(send, recv, mate)

    fa[...] = jnp.zeros_like(fa)
    fb[...] = jnp.zeros_like(fb)

    barrier = pltpu.get_barrier_semaphore()

    def greet(j, carry):
        dev, _ = member((pos + j) % MEMBERS)
        pl.semaphore_signal(barrier, inc=1, device_id=dev, device_id_type=MESH)
        return carry

    lax.fori_loop(1, MEMBERS, greet, 0)
    for dev in (device((z + 1) % 4, h, c, y, q), device((z + 3) % 4, h, c, y, q), device(z, 1 - h, c, y, q)):
        pl.semaphore_signal(barrier, inc=1, device_id=dev, device_id_type=MESH)
    pl.semaphore_wait(barrier, MEMBERS + 2)

    def columns(piece, off, width):
        return pl.ds(pl.multiple_of(piece * PIECE + off, 128), width)

    own = []
    for buf, base, off, width, n in ((ra, ID_IN_A, 0, WA, 0), (rb, ID_IN_B, WA, WB, 1)):

        def scatter(j, carry, buf=buf, base=base, off=off, width=width):
            dev, piece = member((pos + j) % MEMBERS)
            net.push(shard.at[:, columns(piece, off, width)], buf.at[pos], base + j, dev)
            return carry

        lax.fori_loop(1, MEMBERS, scatter, 0)
        keep = pltpu.make_async_copy(shard.at[:, columns(k * 2 + c, off, width)], buf.at[pos], local.at[n])
        keep.start()
        own.append(keep)

    first = starts[grp * MEMBERS]
    for s in range(MEMBERS):
        d = grp * MEMBERS + s
        begin = starts[d] - first
        following = starts[jnp.minimum(d + 1, SHARDS - 1)]
        length = jnp.where(d == SHARDS - 1, M, following) - starts[d]
        slot = lax.broadcasted_iota(jnp.int32, (SLOT, WIN), 0)
        place = lax.broadcasted_iota(jnp.int32, (SLOT, WIN), 1)
        hit = (place == slot + begin) & (slot < length)
        unpack[s * SLOT : (s + 1) * SLOT, :] = jnp.where(hit, 1.0, 0.0).astype(jnp.bfloat16)
    for s in range(0, MEMBERS, 2):
        lane = lax.broadcasted_iota(jnp.int32, (WIN, 2 * SLOT), 1)
        place = lax.broadcasted_iota(jnp.int32, (WIN, 2 * SLOT), 0)
        begins, lengths = [], []
        for d in (grp * MEMBERS + s, grp * MEMBERS + s + 1):
            following = starts[jnp.minimum(d + 1, SHARDS - 1)]
            begins.append(starts[d] - first)
            lengths.append(jnp.where(d == SHARDS - 1, M, following) - starts[d])
        upper = lane >= SLOT
        slot = jnp.where(upper, lane - SLOT, lane)
        begin = jnp.where(upper, begins[1], begins[0])
        length = jnp.where(upper, lengths[1], lengths[0])
        hit = (place == slot + begin) & (slot < length)
        pack[:, s * SLOT : (s + 2) * SLOT] = jnp.where(hit, 1.0, 0.0).astype(jnp.bfloat16)

    def x_ref(part, half, ring, pair):
        buf, slot = (xb if part else xa), ring * 2 + pair
        return buf.at[slot] if half is None else buf.at[slot, pl.ds(half * HALF, HALF)]

    gx = Gather(net, ID_X, z, h, x_ref, lambda ring, pair: device(ring, pair, c, y, q))

    for buf, flat, dst, base, width, n, start in ((ra, fa, xa, ID_IN_A, WA, 0, gx.start_a), (rb, fb, xb, ID_IN_B, WB, 1, gx.start_b)):
        own[n].wait()

        def landed(j, carry, buf=buf, base=base):
            net.arrived(buf.at[(pos + MEMBERS - j) % MEMBERS], base + j)
            return carry

        lax.fori_loop(1, MEMBERS, landed, 0)

        def lay(s, carry, buf=buf, flat=flat):
            flat[pl.ds(pl.multiple_of(s * SLOT, SLOT), CAP), :] = buf[s]
            return carry

        lax.fori_loop(0, MEMBERS, lay, 0)
        for lo in range(0, width, 256):
            hi = min(lo + 256, width)
            dst[grp, :, lo:hi] = dot_nn(pack[...], flat[:, lo:hi]).astype(jnp.bfloat16)
        start()

    def block_of(t):
        return ((z + pick(STEP_RING, t)) % 4) * 2 + (h + pick(STEP_PAIR, t)) % 2

    def gram(a, hh):
        rows = pl.ds(pl.multiple_of(hh * HALF, 16), HALF)
        return dot_nt(xa[grp], xa[a, rows]) + dot_nt(xb[grp], xb[a, rows])

    def finish(t):
        a = block_of(t)
        net.arrived(gmate.at[t], ID_MATE + t)
        total = gown[t % 2] + gmate[t].astype(jnp.float32)

        @pl.when(a == k)
        def _():
            rsum[...] = total

        @pl.when(a != k)
        def _():
            rsnd[t] = total.astype(jnp.bfloat16)
            j = (a + 8 - k) % 8
            net.push(rsnd.at[t], rrcv.at[j], ID_RS + j, device(z, h, c, a // 2, a % 2))

    def gram_step(t, carry):
        for i in range(1, 8):
            if i != 2:

                @pl.when(t == i)
                def _(i=i):
                    gx.before(i)

        a = block_of(t)
        gsnd[t] = gram(a, 1 - c).astype(jnp.bfloat16)
        net.push(gsnd.at[t], gmate.at[t], ID_MATE + t, mate)
        gown[t % 2] = gram(a, c)

        @pl.when(t > 0)
        def _():
            finish(t - 1)

        return carry

    lax.fori_loop(0, 8, gram_step, 0)
    finish(7)

    def collect(j, carry):
        net.arrived(rrcv.at[j], ID_RS + j)
        rsum[...] += rrcv[j].astype(jnp.float32)
        return carry

    lax.fori_loop(1, 8, collect, 0)

    g_cuts = {(0, None): (0, 272), (0, 0): (0, 144), (0, 1): (144, 128), (1, None): (272, 208), (1, 0): (272, 112), (1, 1): (384, 96)}

    def gl_ref(part, half, ring, pair):
        lo, n = g_cuts[part, half]
        return gl.at[ring * 2 + pair, pl.ds(lo, n)]

    def halves_ref(buf):
        def ref(part, half, ring, pair):
            lo, n = g_cuts[part, half]
            return buf.at[ring * 2 + pair, c, pl.ds(lo, n)]

        return ref

    over_rows = Gather(net, ID_GL, z, h, gl_ref, lambda ring, pair: device(ring, pair, c, y, q))
    over_cols = Gather(net, ID_GR, y, q, halves_ref(gr), lambda ring, pair: device(z, h, c, ring, pair))

    def column_of(t):
        return ((y + pick(STEP_RING, t)) % 4) * 2 + (q + pick(STEP_PAIR, t)) % 2

    def to_mate(buf, t, base):
        ref = buf.at[column_of(t), c]
        net.push(ref, ref, base + t, mate)

    def from_mate(buf, t, base):
        net.arrived(buf.at[column_of(t), 1 - c], base + t)

    mine = rsum[...].astype(jnp.bfloat16)
    gl[grp] = mine
    gr[k, c] = mine
    over_rows.start_a()
    over_cols.start_a()
    over_rows.start_b()
    over_cols.start_b()
    to_mate(gr, 0, ID_GRM)
    for t in range(1, 8):
        over_rows.before(t)
        over_cols.before(t)
        to_mate(gr, t, ID_GRM)
    for t in range(8):
        from_mate(gr, t, ID_GRM)

    sq[...] = jnp.zeros_like(sq)

    def square(m, carry):
        sq[...] += dot_nn(gr[m, 0], gl[m, 0:HALF]) + dot_nn(gr[m, 1], gl[m, HALF:WIN])
        return carry

    lax.fori_loop(0, 8, square, 0)
    pb[k, c] = (coef_two * gl[grp].astype(jnp.float32) + coef_three * sq[...]).astype(jnp.bfloat16)

    poly = Gather(net, ID_P, y, q, halves_ref(pb), lambda ring, pair: device(z, h, c, ring, pair))
    poly.start_a()
    poly.start_b()
    acc[...] = jnp.zeros_like(acc)

    def product(t, carry):
        for i in range(1, 8):
            if i != 2:

                @pl.when(t == i)
                def _(i=i):
                    poly.before(i)

        to_mate(pb, t, ID_PM)
        from_mate(pb, t, ID_PM)
        m = column_of(t)
        for lo, hi, buf, off in ((0, WA, xa, 0), (WA, PIECE, xb, WA)):
            acc[:, lo:hi] += dot_nn(pb[m, 0], buf[m, 0:HALF, :]) + dot_nn(pb[m, 1], buf[m, HALF:WIN, :])
        return carry

    lax.fori_loop(0, 8, product, 0)

    for src, stage, base, off, width, n in ((xa, sa, ID_OUT_A, 0, WA, 0), (xb, sb, ID_OUT_B, WA, WB, 1)):
        for lo in range(0, width, 256):
            hi = min(lo + 256, width)
            update = math.sqrt(N) * (coef_one * src[grp, :, lo:hi].astype(jnp.float32) + acc[:, off + lo : off + hi])
            rows = dot_nn(unpack[...], update.astype(jnp.bfloat16)).astype(jnp.bfloat16)
            for s in range(MEMBERS):
                stage[s, :, lo:hi] = rows[s * SLOT : s * SLOT + CAP]

        def give_back(j, carry, stage=stage, base=base, off=off, width=width):
            p = (pos + j) % MEMBERS
            dev, _ = member(p)
            net.push(stage.at[p], out.at[:, columns(k * 2 + c, off, width)], base + j, dev)
            return carry

        lax.fori_loop(1, MEMBERS, give_back, 0)
        keep = pltpu.make_async_copy(stage.at[pos], out.at[:, columns(k * 2 + c, off, width)], local.at[n])
        keep.start()
        own[n] = keep

    for base, off, width, n, buf in ((ID_OUT_A, 0, WA, 0, ra), (ID_OUT_B, WA, WB, 1, rb)):
        own[n].wait()

        def returned(j, carry, base=base, off=off, width=width):
            _, piece = member((pos + MEMBERS - j) % MEMBERS)
            net.arrived(out.at[:, columns(piece, off, width)], base + j)
            return carry

        lax.fori_loop(1, MEMBERS, returned, 0)

    for base, buf in ((ID_IN_A, ra), (ID_IN_B, rb), (ID_OUT_A, ra), (ID_OUT_B, rb)):

        def left(j, carry, base=base, buf=buf):
            net.sent(buf.at[0], base + j)
            return carry

        lax.fori_loop(1, MEMBERS, left, 0)
    for gather in (gx, over_rows, over_cols, poly):
        gather.drain()

    def left_blocks(t, carry):
        for base in (ID_MATE, ID_GRM, ID_PM):
            net.sent(gsnd.at[0], base + t)

        @pl.when(t > 0)
        def _():
            net.sent(gsnd.at[0], ID_RS + t)

        return carry

    lax.fori_loop(0, 8, left_blocks, 0)


def body(momentum_shards, shard_starts):
    bf16, f32 = jnp.bfloat16, jnp.float32
    vmem = pltpu.VMEM
    return pl.pallas_call(
        kernel,
        out_shape=jax.ShapeDtypeStruct((CAP, N), bf16),
        in_specs=[pl.BlockSpec(memory_space=pltpu.SMEM), pl.BlockSpec(memory_space=pl.ANY)],
        out_specs=pl.BlockSpec(memory_space=pl.ANY),
        scratch_shapes=[
            vmem((MEMBERS, CAP, WA), bf16),
            vmem((MEMBERS, CAP, WB), bf16),
            vmem((SLOTS, WA), bf16),
            vmem((SLOTS, WB), bf16),
            vmem((WIN, SLOTS), bf16),
            vmem((SLOTS, WIN), bf16),
            vmem((GROUPS, WIN, WA), bf16),
            vmem((GROUPS, WIN, WB), bf16),
            vmem((2, WIN, HALF), f32),
            vmem((8, WIN, HALF), bf16),
            vmem((8, WIN, HALF), bf16),
            vmem((8, WIN, HALF), bf16),
            vmem((8, WIN, HALF), bf16),
            vmem((WIN, HALF), f32),
            vmem((8, WIN, HALF), bf16),
            vmem((8, 2, WIN, HALF), bf16),
            vmem((8, 2, WIN, HALF), bf16),
            vmem((WIN, PIECE), f32),
            vmem((WIN, HALF), f32),
            vmem((MEMBERS, CAP, WA), bf16),
            vmem((MEMBERS, CAP, WB), bf16),
            pltpu.SemaphoreType.DMA((IDS,)),
            pltpu.SemaphoreType.DMA((IDS,)),
            pltpu.SemaphoreType.DMA((2,)),
        ],
        compiler_params=pltpu.CompilerParams(collective_id=0, has_side_effects=True, vmem_limit_bytes=62 * 1024 * 1024),
    )(shard_starts, momentum_shards)


def solution(mesh):
    in_specs = (P(("row", "col"), None), P())
    out_specs = P(("row", "col"), None)
    return jax.shard_map(body, mesh=mesh, in_specs=in_specs, out_specs=out_specs, check_vma=False)
```

time: 388 us -> 188 us (0.48)
  waiting for transfers between devices: 196 us -> 0 us
  Pallas kernels: 0 us -> 184 us
  blocking collectives: 114 us -> 0 us
  matrix products: 32 us -> 0 us
  local copies, waits for them, and re-layouts: 22.3 us -> 3.02 us
  between operations: 13.5 us -> 0.01 us
  starting transfers between devices: 6.15 us -> 0 us
    pallas_call x0 -> x1, Pallas kernels: none -> 184 us  [body(): pl.pallas_call(kernel, out_shape=jax.ShapeDtypeStruct((CAP, N), bf16), in...]
    all_gather x2 -> x0, waiting for transfers between devices: 170 us -> none  [the longest x1 118 us: body(): col_panel = lax.all_gather(local_tile, 'row', axis=0, tiled=True)]
    all_to_all x4 -> x0, blocking collectives: 114 us -> none  [the longest x2 59 us: summed_on_arrival(): tiles = lax.all_to_all(in_blocks(value, dim, size), axis, 0, 0, tiled=True)]
    dot_general x4 -> x0, matrix products: 32 us -> none  [the longest x1 12.8 us: body(): lax.dot_general(col_panel, local_tile, (((1,), (1,)), ((), ())), preferre...]
    all_to_all x1 -> x0, waiting for transfers between devices: 25.3 us -> none  [body(): lax.all_to_all(momentum_shards, 'col', split_axis=1, concat_axis=0, tiled...]
    reshape x4 -> x0, local copies, waits for them, and re-layouts: 12.5 us -> none  [in_blocks(): value.reshape(*shape[:dim], size, shape[dim] // size, *shape[dim + 1:])]
    all_to_all x1 -> x0, starting transfers between devices: 6.07 us -> none  [body(): lax.all_to_all(momentum_shards, 'col', split_axis=1, concat_axis=0, tiled...]
    all_to_all x5 -> x0, local copies, waits for them, and re-layouts: 5.18 us -> none  [the longest x3 3.19 us: body(): lax.all_to_all(momentum_shards, 'col', split_axis=1, concat_axis=0, tiled...]
  transfers between devices with their start and end apart: 3 -> 0, of which waited for: 3 -> 0; matrix products, arithmetic and copies ran while one was open for 0% -> 0% of each run, Pallas kernels for 0% -> 0%
where the time goes in v1:
time: 188 us; the launch traced here: 187 us
  Pallas kernels  184 us (98%)
  local copies, waits for them, and re-layouts  3.02 us (2%)
    pallas_call x1, Pallas kernels, body(): pl.pallas_call(kernel, out_shape=jax.ShapeDtypeStruct((CAP, N), bf16), in...  184 us

profile of v1, /device:TPU:1, one launch (start us, length us, event | category | flops | bytes accessed | tf_op | source)
XLA Modules:
  0.0 186.7 jit_solution(8058845153808588851)
XLA Ops:
  0.0 183.7 %shard_map.28 = bf16[52,18432]{1,0:T(8,128)(2,1)} custom-call(s32[128]{0:T(128)} %starts.1, bf16[52,18432]{1,0:T(8,128)(2,1)} %shard.1), custom_call_target="tpu_custom_call" | custom-call | tf_op jit(solution)/shard_map/pallas_call | solution.py:448
  183.7 3.0 %copy.4 = bf16[52,18432]{1,0:T(8,128)(2,1)} copy(bf16[52,18432]{1,0:T(8,128)(2,1)} %shard_map.28) | data formatting | bytes 3833856
